TPU v7x, 32 devices: a whole 2x2x4 slice. The times are simulated.
32 devices in a mesh: group: 2 (over x), rows: 16 (over z, y, core).
Axes of the slice: x: 2, y: 2, z: 4, core: 2. Of those that a mesh axis runs over, the one named last changes fastest.
Arguments:
- queries: bfloat16 [256, 3072], P(('group', 'rows')), parts along dimension 0, may hold values from -200 to 200
- prefix_keys: bfloat16 [2048, 1024], P(('group', 'rows')), parts along dimension 0, may hold values from -6 to 6
- prefix_values: bfloat16 [2048, 1024], P(('group', 'rows')), parts along dimension 0, may hold values from -6 to 6
- tree_keys: bfloat16 [256, 1024], P(('group', 'rows')), parts along dimension 0, may hold values from -12 to 12
- tree_values: bfloat16 [256, 1024], P(('group', 'rows')), parts along dimension 0, may hold values from -6 to 6
- parents: int32 [256], P('group'), parts along dimension 0, may hold values from 0 to 95, as said below
Outputs:
- attended: bfloat16 [256, 3072], P(('group', 'rows')), parts along dimension 0
There are 2 independent parts, one for each index of `group`. A program takes and returns all parts, laid end to end along the dimension named above; each array names one. Nothing has to cross between parts.
Inputs may be any that keep to these rules, and one draw needn't show every extreme that they name: `parents`: the rows hold the candidate trees of many requests, in 4 levels of 32 rows in order; a row of the first level is a tree's root and its own parent; every other row's parent is a row of the level before its own, and the first and the last row of each later level have the last row of the level before as parent.
All inputs are finite; a program needn't handle non-finite values.
Results may differ from a plain program's by a relative error of at most 0.005.
Values may be sent and summed in bfloat16 or wider, within the bound.
A program may use at most 192 MiB of HBM per device.

v0:
```python
import jax
import jax.numpy as jnp
from jax import lax
from jax.sharding import PartitionSpec as P

QUERY_HEADS = 24
KV_HEADS = 8
HEAD_DIM = 128
TREE_DEPTH = 4


def as_sent(x):

    def short(part):
        return part.astype(jnp.bfloat16) if part.dtype == jnp.float32 else part

    return jax.tree.map(short, x)


def partner(x, axis, bit):
    return lax.ppermute(x, axis, [(i, i ^ 1 << bit) for i in range(lax.axis_size(axis))])


def lineage_mask(parents, row_ids):
    walker = row_ids
    columns = jnp.arange(parents.shape[0], dtype=jnp.int32)
    allowed = walker[:, None] == columns[None, :]
    for level_step in range(TREE_DEPTH - 1):
        walker = parents[walker]
        allowed = allowed | (walker[:, None] == columns[None, :])
    return allowed


def empty_stats(count):
    groups = QUERY_HEADS // KV_HEADS
    maxima = jnp.full((count, KV_HEADS, groups), -jnp.inf, jnp.float32)
    masses = jnp.zeros((count, KV_HEADS, groups), jnp.float32)
    weighted = jnp.zeros((count, KV_HEADS, groups, HEAD_DIM), jnp.float32)
    return (maxima, masses, weighted)


def score_tile(query_rows, key_tile):
    key_heads = key_tile.reshape(-1, KV_HEADS, HEAD_DIM)
    scores = jnp.einsum("rkgd,nkd->rkgn", query_rows, key_heads, preferred_element_type=jnp.float32)
    return scores * HEAD_DIM ** (-0.5)


def absorb(running, query_rows, key_tile, value_tile, allowed):
    maxima, masses, weighted = running
    scores = score_tile(query_rows, key_tile)
    scores = jnp.where(allowed[:, None, None, :], scores, -jnp.inf)
    raised = jnp.max(scores, axis=-1)
    shrink = jnp.exp(maxima - raised)
    weights = jnp.exp(scores - raised[..., None])
    masses = masses * shrink + jnp.sum(weights, axis=-1)
    value_heads = value_tile.reshape(-1, KV_HEADS, HEAD_DIM)
    update = jnp.einsum(
        "rkgn,nkd->rkgd",
        weights.astype(jnp.bfloat16),
        value_heads,
        preferred_element_type=jnp.float32,
    )
    weighted = weighted * shrink[..., None] + update
    return (raised, masses, weighted)


def empty_head(count):
    groups = QUERY_HEADS // KV_HEADS
    maxima = jnp.full((count, groups), -jnp.inf, jnp.float32)
    masses = jnp.zeros((count, groups), jnp.float32)
    weighted = jnp.zeros((count, groups, HEAD_DIM), jnp.float32)
    return (maxima, masses, weighted)


def absorb_head(running, query_rows, key_tile, value_tile):
    maxima, masses, weighted = running
    scores = jnp.einsum(
        "rgd,nd->rgn", query_rows, key_tile, preferred_element_type=jnp.float32
    ) * HEAD_DIM ** (-0.5)
    raised = jnp.maximum(maxima, jnp.max(scores, axis=-1))
    shrink = jnp.exp(maxima - raised)
    weights = jnp.exp(scores - raised[..., None])
    masses = masses * shrink + jnp.sum(weights, axis=-1)
    update = jnp.einsum(
        "rgn,nd->rgd", weights.astype(jnp.bfloat16), value_tile, preferred_element_type=jnp.float32
    )
    weighted = weighted * shrink[..., None] + update
    return (raised, masses, weighted)


def combine_stats(left, right):
    maxima = jnp.maximum(left[0], right[0])
    left_factor = jnp.exp(left[0] - maxima)
    right_factor = jnp.exp(right[0] - maxima)
    masses = left[1] * left_factor + right[1] * right_factor
    weighted = left[2] * left_factor[..., None] + right[2] * right_factor[..., None]
    return (maxima, masses, weighted)


def head_transpose(members, position, mover):
    slot_count = members[0].shape[0]
    bit_count = slot_count.bit_length() - 1
    for level_bit in range(bit_count):
        own_bit = position // 2**level_bit % 2
        kept_list = []
        sent_list = []
        for member in members:
            shaped = member.reshape(
                (slot_count // 2 ** (level_bit + 1), 2, 2**level_bit) + member.shape[1:]
            )
            lower_half = shaped[:, 0]
            upper_half = shaped[:, 1]
            kept_list.append(jnp.where(own_bit == 0, lower_half, upper_half))
            sent_list.append(jnp.where(own_bit == 0, upper_half, lower_half))
        received = mover(tuple(sent_list), level_bit)
        fresh = []
        for kept, arrived, member in zip(kept_list, received, members):
            first_half = jnp.where(own_bit == 0, kept, arrived)
            second_half = jnp.where(own_bit == 0, arrived, kept)
            fresh.append(jnp.stack([first_half, second_half], axis=1).reshape(member.shape))
        members = tuple(fresh)
    return members


def shards(queries, prefix_keys, prefix_values, tree_keys, tree_values, parents):
    groups = QUERY_HEADS // KV_HEADS
    local_rows = queries.shape[0]
    query_rows = queries.reshape(local_rows, KV_HEADS, groups, HEAD_DIM)
    every_tree_key, every_tree_value = (
        lax.all_gather(tree_keys, "rows", axis=0, tiled=True),
        lax.all_gather(tree_values, "rows", axis=0, tiled=True),
    )
    first_row = lax.axis_index("rows") * local_rows
    row_ids = first_row + jnp.arange(local_rows, dtype=jnp.int32)
    allowed = lineage_mask(parents, row_ids)
    tree_stats = absorb(
        empty_stats(local_rows), query_rows, every_tree_key, every_tree_value, allowed
    )
    position = lax.axis_index("rows")
    head_queries = jnp.transpose(
        queries.reshape(local_rows, KV_HEADS, groups * HEAD_DIM), (1, 0, 2)
    )
    head_keys = jnp.transpose(prefix_keys.reshape(-1, KV_HEADS, HEAD_DIM), (1, 0, 2))
    head_values = jnp.transpose(prefix_values.reshape(-1, KV_HEADS, HEAD_DIM), (1, 0, 2))

    def inward(sent, level_bit):
        return jax.tree.map(
            lambda part, own: part.astype(own.dtype),
            partner(as_sent(sent), "rows", level_bit),
            sent,
        )

    head_queries, head_keys, head_values = head_transpose(
        (head_queries, head_keys, head_values), position, inward
    )
    block_rows = KV_HEADS * local_rows
    my_queries = head_queries.reshape(block_rows, groups, HEAD_DIM)
    slab_keys = head_keys.reshape(-1, HEAD_DIM)
    slab_values = head_values.reshape(-1, HEAD_DIM)
    running = absorb_head(empty_head(block_rows), my_queries, slab_keys, slab_values)
    low_bits = KV_HEADS.bit_length() - 1
    all_bits = lax.axis_size("rows").bit_length() - 1
    for level_bit in range(low_bits, all_bits):
        far_keys, far_values = partner((slab_keys, slab_values), "rows", level_bit)
        running = absorb_head(running, my_queries, far_keys, far_values)
        if level_bit + 1 < all_bits:
            slab_keys = jnp.concatenate([slab_keys, far_keys], axis=0)
            slab_values = jnp.concatenate([slab_values, far_values], axis=0)
    shaped = (
        running[0].reshape(KV_HEADS, local_rows, groups),
        running[1].reshape(KV_HEADS, local_rows, groups),
        running[2].reshape(KV_HEADS, local_rows, groups, HEAD_DIM),
    )

    def outward(sent, level_bit):
        return partner(sent, "rows", level_bit)

    returned = head_transpose(shaped, position, outward)
    owned = (
        jnp.transpose(returned[0], (1, 0, 2)),
        jnp.transpose(returned[1], (1, 0, 2)),
        jnp.transpose(returned[2], (1, 0, 2, 3)),
    )
    final = combine_stats(tree_stats, owned)
    result = final[2] / final[1][..., None]
    return result.reshape(local_rows, QUERY_HEADS * HEAD_DIM).astype(jnp.bfloat16)


def solution(mesh):
    placed = (
        P(("group", "rows"), None),
        P(("group", "rows"), None),
        P(("group", "rows"), None),
        P(("group", "rows"), None),
        P(("group", "rows"), None),
        P("group"),
    )
    return jax.shard_map(
        shards, mesh=mesh, in_specs=placed, out_specs=P(("group", "rows"), None), check_vma=False
    )
```

profile of v0, /device:TPU:0, one launch (start us, length us, event | category | flops | bytes accessed | tf_op | source)
XLA Modules:
  0.0 93.2 jit_solution(2986927178429913200)
XLA Ops:
  0.0 0.9 %copy.258 = bf16[8,8,8,128]{3,2,1,0:T(8,128)(2,1)S(1)} copy(bf16[8,8,8,128]{3,1,2,0:T(8,128)(2,1)} %bitcast.540) | data formatting | bytes 262144
  1.0 0.6 collective-permute-start.10
  2.0 0.6 collective-permute-start.3
  2.7 0.6 collective-permute-start
  3.5 23.8 %all_gather.6 = bf16[128,1024]{1,0:T(8,128)(2,1)S(1)} all-gather(bf16[8,1024]{1,0:T(8,128)(2,1)S(1)} %copy-done.3), channel_id=1, replica_groups=mesh['group'=2,'rows'=16] {'rows'}, dimensions={0}, use_global_device_ids=true | all-gather | bytes 278528 | tf_op jit(solution)/shard_map/all_gather | solution.py:130
  27.5 0.6 gather_fusion
  28.1 0.6 gather_fusion.1
  28.8 0.6 gather_fusion.2
  30.2 0.6 copy-done.4
  30.8 19.3 %all_gather.7 = bf16[128,1024]{1,0:T(8,128)(2,1)S(1)} all-gather(bf16[8,1024]{1,0:T(8,128)(2,1)S(1)} %copy-done.4), channel_id=1, replica_groups=mesh['group'=2,'rows'=16] {'rows'}, dimensions={0}, use_global_device_ids=true | all-gather | bytes 278528 | tf_op jit(solution)/shard_map/all_gather | solution.py:131
  50.5 0.6 collective-permute-start.11
  51.1 1.6 %collective-permute-start.4 = (bf16[2,2,64,128]{3,2,0,1:T(8,128)(2,1)S(1)}, bf16[2,2,64,128]{3,2,0,1:T(8,128)(2,1)S(1)}, u32[]{:S(2)}, u32[]{:S(2)}) collective-permute-start(bf16[2,2,64,128]{3,2,0,1:T(8,128)(2,1)S(1)} %fusion.21), channel_id=1, source_target_pairs={{0,2},{1,3},{2,0},{3,1},{4,6},{5,7},{6,4},{7,5},{8,10},{9,11},{10,... | collective-permute-start | bytes 196616 | tf_op jit(solution)/shard_map/ppermute | solution.py:21
  52.7 1.6 %collective-permute-done.2 = bf16[1,4,8,384]{3,2,1,0:T(8,128)(2,1)S(1)} collective-permute-done((bf16[1,4,8,384]{3,2,1,0:T(8,128)(2,1)S(1)}, bf16[1,4,8,384]{3,2,1,0:T(8,128)(2,1)S(1)}, u32[]{:S(2)}, u32[]{:S(2)}) %collective-permute-start.2) | collective-permute-done | bytes 24608 | tf_op jit(solution)/shard_map/ppermute | solution.py:21
  54.3 2.0 %collective-permute-done.4 = bf16[2,2,64,128]{3,2,0,1:T(8,128)(2,1)S(1)} collective-permute-done((bf16[2,2,64,128]{3,2,0,1:T(8,128)(2,1)S(1)}, bf16[2,2,64,128]{3,2,0,1:T(8,128)(2,1)S(1)}, u32[]{:S(2)}, u32[]{:S(2)}) %collective-permute-start.4) | collective-permute-done | bytes 65568 | tf_op jit(solution)/shard_map/ppermute | solution.py:21
  56.3 1.8 %collective-permute-start.5 = (bf16[1,4,64,128]{3,2,1,0:T(8,128)(2,1)S(1)}, bf16[1,4,64,128]{3,2,1,0:T(8,128)(2,1)S(1)}, u32[]{:S(2)}, u32[]{:S(2)}) collective-permute-start(bf16[1,4,64,128]{3,2,1,0:T(8,128)(2,1)S(1)} %select_bitcast_fusion.3), channel_id=1, source_target_pairs={{0,4},{1,5},{2,6},{3,7},{4,0},{5,1},{6,2},{7,3},{8,12},{9,13},{10,... | collective-permute-start | bytes 196616 | tf_op jit(solution)/shard_map/ppermute | solution.py:21
  58.6 2.6 %collective-permute-done.5 = bf16[1,4,64,128]{3,2,1,0:T(8,128)(2,1)S(1)} collective-permute-done((bf16[1,4,64,128]{3,2,1,0:T(8,128)(2,1)S(1)}, bf16[1,4,64,128]{3,2,1,0:T(8,128)(2,1)S(1)}, u32[]{:S(2)}, u32[]{:S(2)}) %collective-permute-start.5) | collective-permute-done | bytes 65568 | tf_op jit(solution)/shard_map/ppermute | solution.py:21
  61.3 1.2 %collective-permute-done.12 = bf16[1,4,64,128]{3,2,1,0:T(8,128)(2,1)S(1)} collective-permute-done((bf16[1,4,64,128]{3,2,1,0:T(8,128)(2,1)S(1)}, bf16[1,4,64,128]{3,2,1,0:T(8,128)(2,1)S(1)}, u32[]{:S(2)}, u32[]{:S(2)}) %collective-permute-start.12) | collective-permute-done | bytes 65568 | tf_op jit(solution)/shard_map/ppermute | solution.py:21
  62.6 1.8 %collective-permute-start.13 = (bf16[512,128]{1,0:T(8,128)(2,1)S(1)}, bf16[512,128]{1,0:T(8,128)(2,1)S(1)}, u32[]{:S(2)}, u32[]{:S(2)}) collective-permute-start(bf16[512,128]{1,0:T(8,128)(2,1)S(1)} %bitcast.522), channel_id=1, source_target_pairs={{0,8},{1,9},{2,10},{3,11},{4,12},{5,13},{6,14},{7,15},{8,0},{9,1},... | collective-permute-start | bytes 393224 | tf_op jit(solution)/shard_map/ppermute | solution.py:21
  65.0 7.0 %collective-permute-done.6 = bf16[512,128]{1,0:T(8,128)(2,1)S(1)} collective-permute-done((bf16[512,128]{1,0:T(8,128)(2,1)S(1)}, bf16[512,128]{1,0:T(8,128)(2,1)S(1)}, u32[]{:S(2)}, u32[]{:S(2)}) %collective-permute-start.6) | collective-permute-done | bytes 131104 | tf_op jit(solution)/shard_map/ppermute | solution.py:21
  72.9 1.0 %collective-permute-done.13 = bf16[512,128]{1,0:T(8,128)(2,1)S(1)} collective-permute-done((bf16[512,128]{1,0:T(8,128)(2,1)S(1)}, bf16[512,128]{1,0:T(8,128)(2,1)S(1)}, u32[]{:S(2)}, u32[]{:S(2)}) %collective-permute-start.13) | collective-permute-done | bytes 131104 | tf_op jit(solution)/shard_map/ppermute | solution.py:21
  74.3 0.6 collective-permute-start.17
  75.0 0.7 collective-permute-done.17
  76.3 1.7 %collective-permute-start.8 = (f32[2,2,8,3]{2,1,3,0:T(2,128)S(1)}, f32[2,2,8,3]{2,1,3,0:T(2,128)S(1)}, u32[]{:S(2)}, u32[]{:S(2)}) collective-permute-start(f32[2,2,8,3]{2,1,3,0:T(2,128)S(1)} %bitcast.559), channel_id=1, source_target_pairs={{0,2},{1,3},{2,0},{3,1},{4,6},{5,7},{6,4},{7,5},{8,10},{9,11},{10,... | collective-permute-start | bytes 1160 | tf_op jit(solution)/shard_map/ppermute | solution.py:21
  78.0 1.5 %collective-permute-done.18 = f32[2,2,8,3]{2,1,3,0:T(2,128)S(1)} collective-permute-done((f32[2,2,8,3]{2,1,3,0:T(2,128)S(1)}, f32[2,2,8,3]{2,1,3,0:T(2,128)S(1)}, u32[]{:S(2)}, u32[]{:S(2)}) %collective-permute-start.18) | collective-permute-done | bytes 416 | tf_op jit(solution)/shard_map/ppermute | solution.py:21
  80.1 1.7 %collective-permute-start.9 = (f32[1,4,8,3]{2,1,3,0:T(4,128)S(1)}, f32[1,4,8,3]{2,1,3,0:T(4,128)S(1)}, u32[]{:S(2)}, u32[]{:S(2)}) collective-permute-start(f32[1,4,8,3]{2,1,3,0:T(4,128)S(1)} %select_bitcast_fusion.13), channel_id=1, source_target_pairs={{0,4},{1,5},{2,6},{3,7},{4,0},{5,1},{6,2},{7,3},{8,12},{9,13},{10,... | collective-permute-start | bytes 1160 | tf_op jit(solution)/shard_map/ppermute | solution.py:21
  81.8 1.5 %collective-permute-done.19 = f32[1,4,8,3]{2,1,3,0:T(4,128)S(1)} collective-permute-done((f32[1,4,8,3]{2,1,3,0:T(4,128)S(1)}, f32[1,4,8,3]{2,1,3,0:T(4,128)S(1)}, u32[]{:S(2)}, u32[]{:S(2)}) %collective-permute-start.19) | collective-permute-done | bytes 416 | tf_op jit(solution)/shard_map/ppermute | solution.py:21
  83.2 0.5 collective-permute-done.9
  83.8 1.7 %collective-permute-start.15 = (f32[2,2,8,3,128]{4,2,3,1,0:T(8,128)S(1)}, f32[2,2,8,3,128]{4,2,3,1,0:T(8,128)S(1)}, u32[]{:S(2)}, u32[]{:S(2)}) collective-permute-start(f32[2,2,8,3,128]{4,2,3,1,0:T(8,128)S(1)} %select_bitcast_fusion.7), channel_id=1, source_target_pairs={{0,2},{1,3},{2,0},{3,1},{4,6},{5,7},{6,4},{7,5},{8,10},{9,11},{10,... | collective-permute-start | bytes 147464 | tf_op jit(solution)/shard_map/ppermute | solution.py:21
  85.6 2.4 %collective-permute-done.15 = f32[2,2,8,3,128]{4,2,3,1,0:T(8,128)S(1)} collective-permute-done((f32[2,2,8,3,128]{4,2,3,1,0:T(8,128)S(1)}, f32[2,2,8,3,128]{4,2,3,1,0:T(8,128)S(1)}, u32[]{:S(2)}, u32[]{:S(2)}) %collective-permute-start.15) | collective-permute-done | bytes 49184 | tf_op jit(solution)/shard_map/ppermute | solution.py:21
  88.0 1.7 %collective-permute-start.16 = (f32[1,4,8,3,128]{4,2,3,1,0:T(8,128)S(1)}, f32[1,4,8,3,128]{4,2,3,1,0:T(8,128)S(1)}, u32[]{:S(2)}, u32[]{:S(2)}) collective-permute-start(f32[1,4,8,3,128]{4,2,3,1,0:T(8,128)S(1)} %select_bitcast_fusion.6), channel_id=1, source_target_pairs={{0,4},{1,5},{2,6},{3,7},{4,0},{5,1},{6,2},{7,3},{8,12},{9,13},{10,... | collective-permute-start | bytes 147464 | tf_op jit(solution)/shard_map/ppermute | solution.py:21
  89.8 2.4 %collective-permute-done.16 = f32[1,4,8,3,128]{4,2,3,1,0:T(8,128)S(1)} collective-permute-done((f32[1,4,8,3,128]{4,2,3,1,0:T(8,128)S(1)}, f32[1,4,8,3,128]{4,2,3,1,0:T(8,128)S(1)}, u32[]{:S(2)}, u32[]{:S(2)}) %collective-permute-start.16) | collective-permute-done | bytes 49184 | tf_op jit(solution)/shard_map/ppermute | solution.py:21
  92.3 0.9 fusion.7
  (112 shorter events, 6.0 us)
Async XLA Ops:
  0.0 27.5 %copy-start = (s32[128]{0:T(128)S(1)}, s32[128]{0:T(128)}, u32[]{:S(2)}) copy-start(s32[128]{0:T(128)} %param.11) | copy-start | bytes 1540
  1.0 0.9 copy-start.2
  1.0 49.4 %collective-permute-start.10 = (bf16[4,1,64,128]{3,2,0,1:T(8,128)(2,1)S(1)}, bf16[4,1,64,128]{3,2,0,1:T(8,128)(2,1)S(1)}, u32[]{:S(2)}, u32[]{:S(2)}) collective-permute-start(bf16[4,1,64,128]{3,2,0,1:T(8,128)(2,1)S(1)} %select_bitcast_fusion.2), channel_id=1, source_target_pairs={{0,1},{1,0},{2,3},{3,2},{4,5},{5,4},{6,7},{7,6},{8,9},{9,8},{10,11... | collective-permute-start | bytes 196616 | tf_op jit(solution)/shard_map/ppermute | solution.py:21
  1.9 0.8 copy-start.1
  2.0 49.1 %collective-permute-start.3 = (bf16[4,1,64,128]{3,2,0,1:T(8,128)(2,1)S(1)}, bf16[4,1,64,128]{3,2,0,1:T(8,128)(2,1)S(1)}, u32[]{:S(2)}, u32[]{:S(2)}) collective-permute-start(bf16[4,1,64,128]{3,2,0,1:T(8,128)(2,1)S(1)} %fusion.20), channel_id=1, source_target_pairs={{0,1},{1,0},{2,3},{3,2},{4,5},{5,4},{6,7},{7,6},{8,9},{9,8},{10,11... | collective-permute-start | bytes 196616 | tf_op jit(solution)/shard_map/ppermute | solution.py:21
  2.7 0.7 copy-start.3
  2.7 27.3 %collective-permute-start = (bf16[4,1,8,384]{3,2,0,1:T(8,128)(2,1)S(1)}, bf16[4,1,8,384]{3,2,0,1:T(8,128)(2,1)S(1)}, u32[]{:S(2)}, u32[]{:S(2)}) collective-permute-start(bf16[4,1,8,384]{3,2,0,1:T(8,128)(2,1)S(1)} %fusion.44), channel_id=1, source_target_pairs={{0,1},{1,0},{2,3},{3,2},{4,5},{5,4},{6,7},{7,6},{8,9},{9,8},{10,11... | collective-permute-start | bytes 73736 | tf_op jit(solution)/shard_map/ppermute | solution.py:21
  30.1 0.7 copy-start.4
  30.1 20.2 %collective-permute-start.1 = (bf16[2,2,8,384]{3,2,0,1:T(8,128)(2,1)S(1)}, bf16[2,2,8,384]{3,2,0,1:T(8,128)(2,1)S(1)}, u32[]{:S(2)}, u32[]{:S(2)}) collective-permute-start(bf16[2,2,8,384]{3,2,0,1:T(8,128)(2,1)S(1)} %fusion.45), channel_id=1, source_target_pairs={{0,2},{1,3},{2,0},{3,1},{4,6},{5,7},{6,4},{7,5},{8,10},{9,11},{10,... | collective-permute-start | bytes 73736 | tf_op jit(solution)/shard_map/ppermute | solution.py:21
  50.3 3.9 %collective-permute-start.2 = (bf16[1,4,8,384]{3,2,1,0:T(8,128)(2,1)S(1)}, bf16[1,4,8,384]{3,2,1,0:T(8,128)(2,1)S(1)}, u32[]{:S(2)}, u32[]{:S(2)}) collective-permute-start(bf16[1,4,8,384]{3,2,1,0:T(8,128)(2,1)S(1)} %select_bitcast_fusion.9), channel_id=1, source_target_pairs={{0,4},{1,5},{2,6},{3,7},{4,0},{5,1},{6,2},{7,3},{8,12},{9,13},{10,... | collective-permute-start | bytes 73736 | tf_op jit(solution)/shard_map/ppermute | solution.py:21
  50.5 7.7 %collective-permute-start.11 = (bf16[2,2,64,128]{3,2,0,1:T(8,128)(2,1)S(1)}, bf16[2,2,64,128]{3,2,0,1:T(8,128)(2,1)S(1)}, u32[]{:S(2)}, u32[]{:S(2)}) collective-permute-start(bf16[2,2,64,128]{3,2,0,1:T(8,128)(2,1)S(1)} %select_bitcast_fusion.1), channel_id=1, source_target_pairs={{0,2},{1,3},{2,0},{3,1},{4,6},{5,7},{6,4},{7,5},{8,10},{9,11},{10,... | collective-permute-start | bytes 196616 | tf_op jit(solution)/shard_map/ppermute | solution.py:21
  51.1 5.2 %collective-permute-start.4 = (bf16[2,2,64,128]{3,2,0,1:T(8,128)(2,1)S(1)}, bf16[2,2,64,128]{3,2,0,1:T(8,128)(2,1)S(1)}, u32[]{:S(2)}, u32[]{:S(2)}) collective-permute-start(bf16[2,2,64,128]{3,2,0,1:T(8,128)(2,1)S(1)} %fusion.21), channel_id=1, source_target_pairs={{0,2},{1,3},{2,0},{3,1},{4,6},{5,7},{6,4},{7,5},{8,10},{9,11},{10,... | collective-permute-start | bytes 196616 | tf_op jit(solution)/shard_map/ppermute | solution.py:21
  56.3 4.8 %collective-permute-start.5 = (bf16[1,4,64,128]{3,2,1,0:T(8,128)(2,1)S(1)}, bf16[1,4,64,128]{3,2,1,0:T(8,128)(2,1)S(1)}, u32[]{:S(2)}, u32[]{:S(2)}) collective-permute-start(bf16[1,4,64,128]{3,2,1,0:T(8,128)(2,1)S(1)} %select_bitcast_fusion.3), channel_id=1, source_target_pairs={{0,4},{1,5},{2,6},{3,7},{4,0},{5,1},{6,2},{7,3},{8,12},{9,13},{10,... | collective-permute-start | bytes 196616 | tf_op jit(solution)/shard_map/ppermute | solution.py:21
  58.2 4.3 %collective-permute-start.12 = (bf16[1,4,64,128]{3,2,1,0:T(8,128)(2,1)S(1)}, bf16[1,4,64,128]{3,2,1,0:T(8,128)(2,1)S(1)}, u32[]{:S(2)}, u32[]{:S(2)}) collective-permute-start(bf16[1,4,64,128]{3,2,1,0:T(8,128)(2,1)S(1)} %select_bitcast_fusion), channel_id=1, source_target_pairs={{0,4},{1,5},{2,6},{3,7},{4,0},{5,1},{6,2},{7,3},{8,12},{9,13},{10,... | collective-permute-start | bytes 196616 | tf_op jit(solution)/shard_map/ppermute | solution.py:21
  61.2 10.8 %collective-permute-start.6 = (bf16[512,128]{1,0:T(8,128)(2,1)S(1)}, bf16[512,128]{1,0:T(8,128)(2,1)S(1)}, u32[]{:S(2)}, u32[]{:S(2)}) collective-permute-start(bf16[512,128]{1,0:T(8,128)(2,1)S(1)} %bitcast.526), channel_id=1, source_target_pairs={{0,8},{1,9},{2,10},{3,11},{4,12},{5,13},{6,14},{7,15},{8,0},{9,1},... | collective-permute-start | bytes 393224 | tf_op jit(solution)/shard_map/ppermute | solution.py:21
  62.6 11.3 %collective-permute-start.13 = (bf16[512,128]{1,0:T(8,128)(2,1)S(1)}, bf16[512,128]{1,0:T(8,128)(2,1)S(1)}, u32[]{:S(2)}, u32[]{:S(2)}) collective-permute-start(bf16[512,128]{1,0:T(8,128)(2,1)S(1)} %bitcast.522), channel_id=1, source_target_pairs={{0,8},{1,9},{2,10},{3,11},{4,12},{5,13},{6,14},{7,15},{8,0},{9,1},... | collective-permute-start | bytes 393224 | tf_op jit(solution)/shard_map/ppermute | solution.py:21
  74.1 9.6 %collective-permute-start.14 = (f32[4,1,8,3,128]{4,2,0,3,1:T(8,128)S(1)}, f32[4,1,8,3,128]{4,2,0,3,1:T(8,128)S(1)}, u32[]{:S(2)}, u32[]{:S(2)}) collective-permute-start(f32[4,1,8,3,128]{4,2,0,3,1:T(8,128)S(1)} %select_bitcast_fusion.8), channel_id=1, source_target_pairs={{0,1},{1,0},{2,3},{3,2},{4,5},{5,4},{6,7},{7,6},{8,9},{9,8},{10,11... | collective-permute-start | bytes 147464 | tf_op jit(solution)/shard_map/ppermute | solution.py:21
  74.3 1.4 %collective-permute-start.17 = (f32[4,1,8,3]{2,0,3,1:T(4,128)S(1)}, f32[4,1,8,3]{2,0,3,1:T(4,128)S(1)}, u32[]{:S(2)}, u32[]{:S(2)}) collective-permute-start(f32[4,1,8,3]{2,0,3,1:T(4,128)S(1)} %bitcast.561), channel_id=1, source_target_pairs={{0,1},{1,0},{2,3},{3,2},{4,5},{5,4},{6,7},{7,6},{8,9},{9,8},{10,11... | collective-permute-start | bytes 1160 | tf_op jit(solution)/shard_map/ppermute | solution.py:21
  74.9 1.3 %collective-permute-start.7 = (f32[4,1,8,3]{2,0,3,1:T(4,128)S(1)}, f32[4,1,8,3]{2,0,3,1:T(4,128)S(1)}, u32[]{:S(2)}, u32[]{:S(2)}) collective-permute-start(f32[4,1,8,3]{2,0,3,1:T(4,128)S(1)} %bitcast.560), channel_id=1, source_target_pairs={{0,1},{1,0},{2,3},{3,2},{4,5},{5,4},{6,7},{7,6},{8,9},{9,8},{10,11... | collective-permute-start | bytes 1160 | tf_op jit(solution)/shard_map/ppermute | solution.py:21
  75.8 3.7 %collective-permute-start.18 = (f32[2,2,8,3]{2,1,3,0:T(2,128)S(1)}, f32[2,2,8,3]{2,1,3,0:T(2,128)S(1)}, u32[]{:S(2)}, u32[]{:S(2)}) collective-permute-start(f32[2,2,8,3]{2,1,3,0:T(2,128)S(1)} %bitcast.558), channel_id=1, source_target_pairs={{0,2},{1,3},{2,0},{3,1},{4,6},{5,7},{6,4},{7,5},{8,10},{9,11},{10,... | collective-permute-start | bytes 1160 | tf_op jit(solution)/shard_map/ppermute | solution.py:21
  76.3 3.7 %collective-permute-start.8 = (f32[2,2,8,3]{2,1,3,0:T(2,128)S(1)}, f32[2,2,8,3]{2,1,3,0:T(2,128)S(1)}, u32[]{:S(2)}, u32[]{:S(2)}) collective-permute-start(f32[2,2,8,3]{2,1,3,0:T(2,128)S(1)} %bitcast.559), channel_id=1, source_target_pairs={{0,2},{1,3},{2,0},{3,1},{4,6},{5,7},{6,4},{7,5},{8,10},{9,11},{10,... | collective-permute-start | bytes 1160 | tf_op jit(solution)/shard_map/ppermute | solution.py:21
  79.5 3.7 %collective-permute-start.19 = (f32[1,4,8,3]{2,1,3,0:T(4,128)S(1)}, f32[1,4,8,3]{2,1,3,0:T(4,128)S(1)}, u32[]{:S(2)}, u32[]{:S(2)}) collective-permute-start(f32[1,4,8,3]{2,1,3,0:T(4,128)S(1)} %select_bitcast_fusion.12), channel_id=1, source_target_pairs={{0,4},{1,5},{2,6},{3,7},{4,0},{5,1},{6,2},{7,3},{8,12},{9,13},{10,... | collective-permute-start | bytes 1160 | tf_op jit(solution)/shard_map/ppermute | solution.py:21
  80.1 3.7 %collective-permute-start.9 = (f32[1,4,8,3]{2,1,3,0:T(4,128)S(1)}, f32[1,4,8,3]{2,1,3,0:T(4,128)S(1)}, u32[]{:S(2)}, u32[]{:S(2)}) collective-permute-start(f32[1,4,8,3]{2,1,3,0:T(4,128)S(1)} %select_bitcast_fusion.13), channel_id=1, source_target_pairs={{0,4},{1,5},{2,6},{3,7},{4,0},{5,1},{6,2},{7,3},{8,12},{9,13},{10,... | collective-permute-start | bytes 1160 | tf_op jit(solution)/shard_map/ppermute | solution.py:21
  83.8 4.2 %collective-permute-start.15 = (f32[2,2,8,3,128]{4,2,3,1,0:T(8,128)S(1)}, f32[2,2,8,3,128]{4,2,3,1,0:T(8,128)S(1)}, u32[]{:S(2)}, u32[]{:S(2)}) collective-permute-start(f32[2,2,8,3,128]{4,2,3,1,0:T(8,128)S(1)} %select_bitcast_fusion.7), channel_id=1, source_target_pairs={{0,2},{1,3},{2,0},{3,1},{4,6},{5,7},{6,4},{7,5},{8,10},{9,11},{10,... | collective-permute-start | bytes 147464 | tf_op jit(solution)/shard_map/ppermute | solution.py:21
  88.0 4.2 %collective-permute-start.16 = (f32[1,4,8,3,128]{4,2,3,1,0:T(8,128)S(1)}, f32[1,4,8,3,128]{4,2,3,1,0:T(8,128)S(1)}, u32[]{:S(2)}, u32[]{:S(2)}) collective-permute-start(f32[1,4,8,3,128]{4,2,3,1,0:T(8,128)S(1)} %select_bitcast_fusion.6), channel_id=1, source_target_pairs={{0,4},{1,5},{2,6},{3,7},{4,0},{5,1},{6,2},{7,3},{8,12},{9,13},{10,... | collective-permute-start | bytes 147464 | tf_op jit(solution)/shard_map/ppermute | solution.py:21
where the time goes:
time: 93.6 us; the launch traced here: 93.2 us
  blocking collectives  43.1 us (46%)
  waiting for transfers between devices  24.8 us (26%)
  starting transfers between devices  16 us (17%)
  local copies, waits for them, and re-layouts  4.99 us (5%)
  matrix products  2.31 us (2%)
  other arithmetic  1.46 us (2%)
    ppermute x20, waiting for transfers between devices, partner(): lax.ppermute(x, axis, [(i, i ^ 1 << bit) for i in range(lax.axis_size(axi...  24.8 us
    all_gather x1, blocking collectives, shards(): lax.all_gather(tree_keys, 'rows', axis=0, tiled=True)  23.8 us
    all_gather x1, blocking collectives, shards(): lax.all_gather(tree_values, 'rows', axis=0, tiled=True)  19.3 us
    ppermute x20, starting transfers between devices, partner(): lax.ppermute(x, axis, [(i, i ^ 1 << bit) for i in range(lax.axis_size(axi...  16 us
    unnamed x12, local copies, waits for them, and re-layouts  2.25 us
    gather x3, local copies, waits for them, and re-layouts, lineage_mask(): walker = parents[walker]  1.93 us
  transfers between devices with their start and end apart: 20, of which 13 were waited for; matrix products, arithmetic and copies ran while one was open for 6% of the time, Pallas kernels for 0%

commit v1 on v0

v1 whole, which is shorter than its diff:
```python
import functools

import jax
import jax.numpy as jnp
from jax import lax
from jax.experimental import pallas as pl
from jax.experimental.pallas import tpu as pltpu
from jax.sharding import PartitionSpec as P

QUERY_HEADS = 24
KV_HEADS = 8
HEAD_DIM = 128
TREE_DEPTH = 4
GROUPS = QUERY_HEADS // KV_HEADS
WIDTH = GROUPS * HEAD_DIM
PART = 32

LAST = (((1,), (1,)), ((), ()))
MESH = pl.DeviceIdType.MESH


def pack_stats(maxima, masses):
    rows = maxima[0].shape[0]
    lane = lax.broadcasted_iota(jnp.int32, (rows, HEAD_DIM), 1)
    place = lane % PART
    stat = jnp.zeros((rows, HEAD_DIM), jnp.float32)
    for at, column in enumerate(maxima + masses):
        stat = jnp.where(place == at, column, stat)
    high = stat.astype(jnp.bfloat16).astype(jnp.float32)
    rest = stat - high
    middle = rest.astype(jnp.bfloat16).astype(jnp.float32)
    low = rest - middle
    return jnp.where(lane < PART, high, jnp.where(lane < 2 * PART, middle, low))


def kernel(
    n, q_in, pk_in, pv_in, tk_in, tv_in, parents, out,
    qbuf, kbuf, vbuf, tbuf, obuf, rbuf, mask,
    sem_q, sem_k, sem_v, sem_t, sem_r, send_q, send_k, send_v, send_t, send_r,
):
    me = lax.axis_index("rows")
    local = q_in.shape[0]
    blocks = n // KV_HEADS
    block_rows = KV_HEADS * local
    my_block = me // KV_HEADS
    my_slot = me % KV_HEADS

    def send(src, dst, send_sem, recv_sem, to):
        pltpu.make_async_remote_copy(
            src_ref=src, dst_ref=dst, send_sem=send_sem, recv_sem=recv_sem,
            device_id={"rows": to}, device_id_type=MESH,
        ).start()

    def settle(ref, sem):
        pltpu.make_async_copy(ref, ref, sem).wait()

    def columns(ref, head, width):
        return ref.at[:, pl.ds(pl.multiple_of(head * width, width), width)]

    barrier = pltpu.get_barrier_semaphore()
    for step in range(1, n):
        pl.semaphore_signal(
            barrier, inc=1, device_id={"rows": (me + step) % n}, device_id_type=MESH
        )
    pltpu.make_async_copy(columns(q_in, my_slot, WIDTH), qbuf.at[me], sem_q.at[my_block]).start()
    pltpu.make_async_copy(columns(pk_in, my_slot, HEAD_DIM), kbuf.at[my_slot], sem_k).start()
    pltpu.make_async_copy(columns(tk_in, my_slot, HEAD_DIM), tbuf.at[0, my_slot], sem_t).start()
    pltpu.make_async_copy(columns(tv_in, my_slot, HEAD_DIM), tbuf.at[1, my_slot], sem_t).start()
    pltpu.make_async_copy(columns(pv_in, my_slot, HEAD_DIM), vbuf.at[my_slot], sem_v).start()
    pl.semaphore_wait(barrier, n - 1)

    for far in range(1, blocks):
        for step in range(KV_HEADS):
            head = (my_slot + step) % KV_HEADS
            to = (my_block + far) % blocks * KV_HEADS + head
            send(columns(q_in, head, WIDTH), qbuf.at[me], send_q, sem_q.at[my_block], to)
    for step in range(1, KV_HEADS):
        head = (my_slot + step) % KV_HEADS
        to = my_block * KV_HEADS + head
        send(columns(q_in, head, WIDTH), qbuf.at[me], send_q, sem_q.at[my_block], to)
        send(columns(tk_in, head, HEAD_DIM), tbuf.at[0, my_slot], send_t, sem_t, to)
        send(columns(pk_in, head, HEAD_DIM), kbuf.at[my_slot], send_k, sem_k, to)
    for step in range(1, KV_HEADS):
        head = (my_slot + step) % KV_HEADS
        to = my_block * KV_HEADS + head
        send(columns(tv_in, head, HEAD_DIM), tbuf.at[1, my_slot], send_t, sem_t, to)
        send(columns(pv_in, head, HEAD_DIM), vbuf.at[my_slot], send_v, sem_v, to)

    count = parents.shape[1]
    parent = jnp.broadcast_to(parents[...], (count, count))
    token = lax.broadcasted_iota(jnp.int32, (count, count), 0)
    row = lax.broadcasted_iota(jnp.int32, (count, count), 1)
    hop = (parent == token).astype(jnp.float32).astype(jnp.bfloat16)
    mine = lax.broadcasted_iota(jnp.int32, (block_rows, count), 0) + my_block * block_rows
    own = lax.broadcasted_iota(jnp.int32, (block_rows, count), 1)
    member = (mine == own).astype(jnp.float32)
    seen = member
    for _ in range(TREE_DEPTH - 1):
        member = jnp.dot(member.astype(jnp.bfloat16), hop, preferred_element_type=jnp.float32)
        seen = seen + member
    same = (token == row).astype(jnp.float32).astype(jnp.bfloat16)
    mask[...] = lax.dot_general(
        same, seen.astype(jnp.bfloat16), LAST, preferred_element_type=jnp.float32
    )

    for order in range(blocks):
        block = (my_block + 1 + order) % blocks
        first = pl.multiple_of(block * KV_HEADS, KV_HEADS)
        settle(qbuf.at[pl.ds(0, KV_HEADS)], sem_q.at[block])
        if order == 0:
            settle(kbuf, sem_k)
            settle(tbuf, sem_t)
            settle(vbuf, sem_v)
        keys = kbuf[...].reshape(-1, HEAD_DIM)
        tree_keys = tbuf[0].astype(jnp.float32).reshape(block_rows, HEAD_DIM).astype(jnp.bfloat16)
        values = vbuf[...].reshape(-1, HEAD_DIM)
        tree_values = tbuf[1].astype(jnp.float32).reshape(block_rows, HEAD_DIM).astype(jnp.bfloat16)
        queries = qbuf[pl.ds(first, KV_HEADS)].astype(jnp.float32).reshape(block_rows, WIDTH)
        visible = mask[pl.ds(pl.multiple_of(block * block_rows, block_rows), block_rows), :] > 0.5
        pieces, maxima, masses = [], [], []
        for group in range(GROUPS):
            query = queries[:, group * HEAD_DIM : (group + 1) * HEAD_DIM].astype(jnp.bfloat16)
            scale = HEAD_DIM ** (-0.5)
            slab = lax.dot_general(query, keys, LAST, preferred_element_type=jnp.float32) * scale
            tree = (
                lax.dot_general(query, tree_keys, LAST, preferred_element_type=jnp.float32) * scale
            )
            tree = jnp.where(visible, tree, -jnp.inf)
            top = jnp.maximum(
                jnp.max(slab, axis=1, keepdims=True), jnp.max(tree, axis=1, keepdims=True)
            )
            slab = jnp.exp(slab - top)
            tree = jnp.exp(tree - top)
            maxima.append(top)
            masses.append(
                jnp.sum(slab, axis=1, keepdims=True) + jnp.sum(tree, axis=1, keepdims=True)
            )
            pieces.append(
                jnp.dot(slab.astype(jnp.bfloat16), values, preferred_element_type=jnp.float32)
                + jnp.dot(
                    tree.astype(jnp.bfloat16), tree_values, preferred_element_type=jnp.float32
                )
            )
        pieces.append(pack_stats(maxima, masses))
        packed = jnp.concatenate(pieces, axis=1).reshape(KV_HEADS, local, WIDTH + HEAD_DIM)
        obuf[pl.ds(first, KV_HEADS)] = packed.astype(jnp.bfloat16)
        for step in range(KV_HEADS):
            if order == blocks - 1 and step == 0:
                pltpu.make_async_copy(obuf.at[me], rbuf.at[me], sem_r).start()
            else:
                to = first + (my_slot + step) % KV_HEADS
                send(obuf.at[to], rbuf.at[me], send_r, sem_r, to)

    settle(qbuf.at[pl.ds(0, n - 1)], send_q)
    settle(kbuf.at[pl.ds(0, KV_HEADS - 1)], send_k)
    settle(vbuf.at[pl.ds(0, KV_HEADS - 1)], send_v)
    settle(tbuf.at[:, pl.ds(0, KV_HEADS - 1)], send_t)
    settle(rbuf, sem_r)

    stat = rbuf[:, :, WIDTH:].astype(jnp.float32).reshape(n * local, HEAD_DIM)
    stat = (
        stat
        + pltpu.roll(stat, HEAD_DIM - PART, 1)
        + pltpu.roll(stat, HEAD_DIM - 2 * PART, 1)
    ).reshape(blocks, block_rows, HEAD_DIM)
    top = jnp.max(stat, axis=0)
    lane = lax.broadcasted_iota(jnp.int32, (block_rows, HEAD_DIM), 1)
    factors = []
    total = jnp.zeros((block_rows, HEAD_DIM), jnp.float32)
    for block in range(blocks):
        factor = jnp.exp(stat[block] - top)
        mass = pltpu.roll(stat[block], HEAD_DIM - GROUPS, 1)
        total = total + factor * mass
        factors.append(factor)
    total = jnp.where(lane < GROUPS, total, 1.0)
    factors = [factor / total for factor in factors]
    for head in range(KV_HEADS):
        for group in range(GROUPS):
            result = jnp.zeros((local, HEAD_DIM), jnp.float32)
            for block in range(blocks):
                share = factors[block][head * local : (head + 1) * local, group : group + 1]
                piece = rbuf[block * KV_HEADS + head, :, group * HEAD_DIM : (group + 1) * HEAD_DIM]
                result = result + piece.astype(jnp.float32) * share
            at = head * WIDTH + group * HEAD_DIM
            out[:, at : at + HEAD_DIM] = result.astype(out.dtype)
    settle(rbuf.at[pl.ds(0, n - 1)], send_r)


def shards(n, queries, prefix_keys, prefix_values, tree_keys, tree_values, parents):
    local = queries.shape[0]
    tokens = prefix_keys.shape[0]
    kind = queries.dtype
    blocks = n // KV_HEADS
    hbm = pl.BlockSpec(memory_space=pl.ANY)
    vmem = pl.BlockSpec(memory_space=pltpu.VMEM)
    dma = pltpu.SemaphoreType.DMA
    return pl.pallas_call(
        functools.partial(kernel, n),
        out_shape=jax.ShapeDtypeStruct(queries.shape, kind),
        in_specs=[hbm] * 5 + [vmem],
        out_specs=vmem,
        scratch_shapes=[
            pltpu.VMEM((n, local, WIDTH), kind),
            pltpu.VMEM((KV_HEADS, tokens, HEAD_DIM), kind),
            pltpu.VMEM((KV_HEADS, tokens, HEAD_DIM), kind),
            pltpu.VMEM((2, KV_HEADS, local, HEAD_DIM), kind),
            pltpu.VMEM((n, local, WIDTH + HEAD_DIM), kind),
            pltpu.VMEM((n, local, WIDTH + HEAD_DIM), kind),
            pltpu.VMEM((n * local, KV_HEADS * local), jnp.float32),
            dma((blocks,)), dma, dma, dma, dma, dma, dma, dma, dma, dma,
        ],
        compiler_params=pltpu.CompilerParams(collective_id=0, has_side_effects=True),
        name="tree_attention",
    )(queries, prefix_keys, prefix_values, tree_keys, tree_values, parents.reshape(1, -1))


def solution(mesh):
    placed = (
        P(("group", "rows"), None),
        P(("group", "rows"), None),
        P(("group", "rows"), None),
        P(("group", "rows"), None),
        P(("group", "rows"), None),
        P("group"),
    )
    return jax.shard_map(
        functools.partial(shards, mesh.shape["rows"]),
        mesh=mesh,
        in_specs=placed,
        out_specs=P(("group", "rows"), None),
        check_vma=False,
    )
```

time: 93.6 us -> 21.8 us (0.23)
  blocking collectives: 43.1 us -> 0 us
  waiting for transfers between devices: 24.8 us -> 0 us
  Pallas kernels: 0 us -> 20.2 us
  starting transfers between devices: 16 us -> 0 us
  local copies, waits for them, and re-layouts: 4.99 us -> 1.42 us
  matrix products: 2.31 us -> 0 us
  other arithmetic: 1.46 us -> 0 us
    all_gather x2 -> x0, blocking collectives: 43.1 us -> none  [the longest x1 23.8 us: shards(): lax.all_gather(tree_keys, 'rows', axis=0, tiled=True)]
    ppermute x20 -> x0, waiting for transfers between devices: 24.8 us -> none  [partner(): lax.ppermute(x, axis, [(i, i ^ 1 << bit) for i in range(lax.axis_size(axi...]
    pallas_call x0 -> x1, Pallas kernels: none -> 20.2 us  [shards(): pl.pallas_call(functools.partial(kernel, n), out_shape=jax.ShapeDtypeStru...]
    ppermute x20 -> x0, starting transfers between devices: 16 us -> none  [partner(): lax.ppermute(x, axis, [(i, i ^ 1 << bit) for i in range(lax.axis_size(axi...]
    dot_general x6 -> x0, matrix products: 2.31 us -> none  [the longest x1 0.92 us: absorb(): jnp.einsum('rkgn,nkd->rkgd', weights.astype(jnp.bfloat16), value_heads, p...]
    gather x3 -> x0, local copies, waits for them, and re-layouts: 1.93 us -> none  [lineage_mask(): walker = parents[walker]]
    unnamed x12 -> x1, local copies, waits for them, and re-layouts: 2.25 us -> 1.42 us
  transfers between devices with their start and end apart: 20 -> 0, of which waited for: 13 -> 0; matrix products, arithmetic and copies ran while one was open for 6% -> 0% of each run, Pallas kernels for 0% -> 0%
where the time goes in v1:
time: 21.8 us; the launch traced here: 21.7 us
  Pallas kernels  20.2 us (93%)
  local copies, waits for them, and re-layouts  1.42 us (7%)
    pallas_call x1, Pallas kernels, shards(): pl.pallas_call(functools.partial(kernel, n), out_shape=jax.ShapeDtypeStru...  20.2 us
    unnamed x1, local copies, waits for them, and re-layouts  1.42 us

profile of v1, /device:TPU:0, one launch (start us, length us, event | category | flops | bytes accessed | tf_op | source)
XLA Modules:
  0.0 21.7 jit_solution(6966204572460241772)
XLA Ops:
  0.0 20.2 %tree_attention.1 = bf16[8,3072]{1,0:T(8,128)(2,1)} custom-call(bf16[8,3072]{1,0:T(8,128)(2,1)} %q_in.1, bf16[64,1024]{1,0:T(8,128)(2,1)} %pk_in.1, bf16[64,1024]{1,0:T(8,128)(2,1)} %pv_in.1, bf16[8,1024]{1,0:T(8,128)(2,1)} %tk_in.1, bf16[8,1024]{1,0:T(8,128)(2,1)} %tv_in.1, s32[1,128]{1,0:T(1,128)} %bitcast.1), custom_call_target="tpu_custom_call" | custom-call | tf_op jit(solution)/shard_map/tree_attention/pallas_call | solution.py:197
  20.2 1.4 %copy.8 = bf16[8,3072]{1,0:T(8,128)(2,1)} copy(bf16[8,3072]{1,0:T(8,128)(2,1)} %tree_attention.1) | data formatting | bytes 98304

commit v2 on v1

--- a/solution.py
+++ b/solution.py
@@ -64,8 +64,8 @@
         )
     pltpu.make_async_copy(columns(q_in, my_slot, WIDTH), qbuf.at[me], sem_q.at[my_block]).start()
     pltpu.make_async_copy(columns(pk_in, my_slot, HEAD_DIM), kbuf.at[my_slot], sem_k).start()
-    pltpu.make_async_copy(columns(tk_in, my_slot, HEAD_DIM), tbuf.at[0, my_slot], sem_t).start()
-    pltpu.make_async_copy(columns(tv_in, my_slot, HEAD_DIM), tbuf.at[1, my_slot], sem_t).start()
+    pltpu.make_async_copy(columns(tk_in, my_slot, HEAD_DIM), tbuf.at[0, my_slot], sem_t.at[0]).start()
+    pltpu.make_async_copy(columns(tv_in, my_slot, HEAD_DIM), tbuf.at[1, my_slot], sem_t.at[1]).start()
     pltpu.make_async_copy(columns(pv_in, my_slot, HEAD_DIM), vbuf.at[my_slot], sem_v).start()
     pl.semaphore_wait(barrier, n - 1)
 
@@ -78,12 +78,12 @@
         head = (my_slot + step) % KV_HEADS
         to = my_block * KV_HEADS + head
         send(columns(q_in, head, WIDTH), qbuf.at[me], send_q, sem_q.at[my_block], to)
-        send(columns(tk_in, head, HEAD_DIM), tbuf.at[0, my_slot], send_t, sem_t, to)
+        send(columns(tk_in, head, HEAD_DIM), tbuf.at[0, my_slot], send_t, sem_t.at[0], to)
         send(columns(pk_in, head, HEAD_DIM), kbuf.at[my_slot], send_k, sem_k, to)
     for step in range(1, KV_HEADS):
         head = (my_slot + step) % KV_HEADS
         to = my_block * KV_HEADS + head
-        send(columns(tv_in, head, HEAD_DIM), tbuf.at[1, my_slot], send_t, sem_t, to)
+        send(columns(tv_in, head, HEAD_DIM), tbuf.at[1, my_slot], send_t, sem_t.at[1], to)
         send(columns(pv_in, head, HEAD_DIM), vbuf.at[my_slot], send_v, sem_v, to)
 
     count = parents.shape[1]
@@ -103,24 +103,20 @@
         same, seen.astype(jnp.bfloat16), LAST, preferred_element_type=jnp.float32
     )
 
-    for order in range(blocks):
-        block = (my_block + 1 + order) % blocks
+    settle(kbuf, sem_k)
+    keys = kbuf[...].reshape(-1, HEAD_DIM)
+    settle(tbuf.at[0], sem_t.at[0])
+    tree_keys = tbuf[0].astype(jnp.float32).reshape(block_rows, HEAD_DIM).astype(jnp.bfloat16)
+    scale = HEAD_DIM ** (-0.5)
+
+    def weigh(block):
         first = pl.multiple_of(block * KV_HEADS, KV_HEADS)
         settle(qbuf.at[pl.ds(0, KV_HEADS)], sem_q.at[block])
-        if order == 0:
-            settle(kbuf, sem_k)
-            settle(tbuf, sem_t)
-            settle(vbuf, sem_v)
-        keys = kbuf[...].reshape(-1, HEAD_DIM)
-        tree_keys = tbuf[0].astype(jnp.float32).reshape(block_rows, HEAD_DIM).astype(jnp.bfloat16)
-        values = vbuf[...].reshape(-1, HEAD_DIM)
-        tree_values = tbuf[1].astype(jnp.float32).reshape(block_rows, HEAD_DIM).astype(jnp.bfloat16)
         queries = qbuf[pl.ds(first, KV_HEADS)].astype(jnp.float32).reshape(block_rows, WIDTH)
         visible = mask[pl.ds(pl.multiple_of(block * block_rows, block_rows), block_rows), :] > 0.5
-        pieces, maxima, masses = [], [], []
+        weights, maxima, masses = [], [], []
         for group in range(GROUPS):
             query = queries[:, group * HEAD_DIM : (group + 1) * HEAD_DIM].astype(jnp.bfloat16)
-            scale = HEAD_DIM ** (-0.5)
             slab = lax.dot_general(query, keys, LAST, preferred_element_type=jnp.float32) * scale
             tree = (
                 lax.dot_general(query, tree_keys, LAST, preferred_element_type=jnp.float32) * scale
@@ -135,21 +131,38 @@
             masses.append(
                 jnp.sum(slab, axis=1, keepdims=True) + jnp.sum(tree, axis=1, keepdims=True)
             )
-            pieces.append(
-                jnp.dot(slab.astype(jnp.bfloat16), values, preferred_element_type=jnp.float32)
-                + jnp.dot(
-                    tree.astype(jnp.bfloat16), tree_values, preferred_element_type=jnp.float32
-                )
-            )
-        pieces.append(pack_stats(maxima, masses))
-        packed = jnp.concatenate(pieces, axis=1).reshape(KV_HEADS, local, WIDTH + HEAD_DIM)
-        obuf[pl.ds(first, KV_HEADS)] = packed.astype(jnp.bfloat16)
+            weights.append((slab.astype(jnp.bfloat16), tree.astype(jnp.bfloat16)))
+        stats = pack_stats(maxima, masses).reshape(KV_HEADS, local, HEAD_DIM)
+        obuf[pl.ds(first, KV_HEADS), :, WIDTH:] = stats.astype(jnp.bfloat16)
+        return weights
+
+    def values_ready():
+        settle(vbuf, sem_v)
+        settle(tbuf.at[1], sem_t.at[1])
+
+    def apply(block, weights, last):
+        first = pl.multiple_of(block * KV_HEADS, KV_HEADS)
+        values = vbuf[...].reshape(-1, HEAD_DIM)
+        tree_values = tbuf[1].astype(jnp.float32).reshape(block_rows, HEAD_DIM).astype(jnp.bfloat16)
+        for group, (slab, tree) in enumerate(weights):
+            piece = jnp.dot(slab, values, preferred_element_type=jnp.float32) + jnp.dot(
+                tree, tree_values, preferred_element_type=jnp.float32
+            )
+            piece = piece.reshape(KV_HEADS, local, HEAD_DIM).astype(jnp.bfloat16)
+            obuf[pl.ds(first, KV_HEADS), :, group * HEAD_DIM : (group + 1) * HEAD_DIM] = piece
         for step in range(KV_HEADS):
-            if order == blocks - 1 and step == 0:
+            if last and step == 0:
                 pltpu.make_async_copy(obuf.at[me], rbuf.at[me], sem_r).start()
             else:
                 to = first + (my_slot + step) % KV_HEADS
                 send(obuf.at[to], rbuf.at[me], send_r, sem_r, to)
+
+    order = [(my_block + 1 + step) % blocks for step in range(blocks)]
+    ahead = [weigh(block) for block in order[:2]]
+    values_ready()
+    for step, block in enumerate(order):
+        weights = ahead[step] if step < 2 else weigh(block)
+        apply(block, weights, step == blocks - 1)
 
     settle(qbuf.at[pl.ds(0, n - 1)], send_q)
     settle(kbuf.at[pl.ds(0, KV_HEADS - 1)], send_k)
@@ -196,7 +209,7 @@
     dma = pltpu.SemaphoreType.DMA
     return pl.pallas_call(
         functools.partial(kernel, n),
-        out_shape=jax.ShapeDtypeStruct(queries.shape, kind),
+        out_shape=pltpu.VMEM(queries.shape, kind),
         in_specs=[hbm] * 5 + [vmem],
         out_specs=vmem,
         scratch_shapes=[
@@ -207,7 +220,7 @@
             pltpu.VMEM((n, local, WIDTH + HEAD_DIM), kind),
             pltpu.VMEM((n, local, WIDTH + HEAD_DIM), kind),
             pltpu.VMEM((n * local, KV_HEADS * local), jnp.float32),
-            dma((blocks,)), dma, dma, dma, dma, dma, dma, dma, dma, dma,
+            dma((blocks,)), dma, dma, dma((2,)), dma, dma, dma, dma, dma, dma,
         ],
         compiler_params=pltpu.CompilerParams(collective_id=0, has_side_effects=True),
         name="tree_attention",

time: 21.8 us -> 19.6 us (0.90)
  Pallas kernels: 20.2 us -> 18.8 us
  local copies, waits for them, and re-layouts: 1.42 us -> 0.62 us
    pallas_call x1, Pallas kernels: 20.2 us -> 18.8 us  [shards(): pl.pallas_call(functools.partial(kernel, n), out_shape=pltpu.VMEM(queries...]
    unnamed x1, local copies, waits for them, and re-layouts: 1.42 us -> 0.62 us
where the time goes in v2:
time: 19.6 us; the launch traced here: 19.4 us
  Pallas kernels  18.8 us (96%)
  local copies, waits for them, and re-layouts  0.62 us (3%)
    pallas_call x1, Pallas kernels, shards(): pl.pallas_call(functools.partial(kernel, n), out_shape=pltpu.VMEM(queries...  18.8 us
    unnamed x1, local copies, waits for them, and re-layouts  0.62 us

profile of v2, /device:TPU:0, one launch (start us, length us, event | category | flops | bytes accessed | tf_op | source)
XLA Modules:
  0.0 19.4 jit_solution(6286618663314197920)
XLA Ops:
  0.0 18.8 %tree_attention.1 = bf16[8,3072]{1,0:T(8,128)(2,1)S(1)} custom-call(bf16[8,3072]{1,0:T(8,128)(2,1)} %q_in.1, bf16[64,1024]{1,0:T(8,128)(2,1)} %pk_in.1, bf16[64,1024]{1,0:T(8,128)(2,1)} %pv_in.1, bf16[8,1024]{1,0:T(8,128)(2,1)} %tk_in.1, bf16[8,1024]{1,0:T(8,128)(2,1)} %tv_in.1, s32[1,128]{1,0:T(1,128)} %bitcast.1), custom_call_target="tpu_custom_call" | custom-call | tf_op jit(solution)/shard_map/tree_attention/pallas_call | solution.py:210
  18.8 0.6 %copy.8 = bf16[8,3072]{1,0:T(8,128)(2,1)} copy(bf16[8,3072]{1,0:T(8,128)(2,1)S(1)} %tree_attention.1) | data formatting | bytes 98304

commit v3 on v2

--- a/solution.py
+++ b/solution.py
@@ -34,9 +34,9 @@
 
 
 def kernel(
-    n, q_in, pk_in, pv_in, tk_in, tv_in, parents, out,
-    qbuf, kbuf, vbuf, tbuf, obuf, rbuf, mask,
-    sem_q, sem_k, sem_v, sem_t, sem_r, send_q, send_k, send_v, send_t, send_r,
+    n, q_in, pk_in, pv_in, tk_in, tv_in, parents_in, out,
+    qbuf, kbuf, vbuf, tbuf, obuf, rbuf, mask, parents,
+    sem_p, far_ready, sem_q, sem_k, sem_v, sem_t, sem_r, send_q, send_k, send_v, send_t, send_r,
 ):
     me = lax.axis_index("rows")
     local = q_in.shape[0]
@@ -58,34 +58,43 @@
         return ref.at[:, pl.ds(pl.multiple_of(head * width, width), width)]
 
     barrier = pltpu.get_barrier_semaphore()
-    for step in range(1, n):
-        pl.semaphore_signal(
-            barrier, inc=1, device_id={"rows": (me + step) % n}, device_id_type=MESH
-        )
+
+    def greet(sem, to):
+        pl.semaphore_signal(sem, inc=1, device_id={"rows": to}, device_id_type=MESH)
+
+    others = [(my_block + far) % blocks for far in range(1, blocks)]
+    heads = [(my_slot + step) % KV_HEADS for step in range(KV_HEADS)]
+    for block in others:
+        greet(barrier, block * KV_HEADS + my_slot)
+    for head in heads[1:]:
+        greet(barrier, my_block * KV_HEADS + head)
     pltpu.make_async_copy(columns(q_in, my_slot, WIDTH), qbuf.at[me], sem_q.at[my_block]).start()
     pltpu.make_async_copy(columns(pk_in, my_slot, HEAD_DIM), kbuf.at[my_slot], sem_k).start()
     pltpu.make_async_copy(columns(tk_in, my_slot, HEAD_DIM), tbuf.at[0, my_slot], sem_t.at[0]).start()
     pltpu.make_async_copy(columns(tv_in, my_slot, HEAD_DIM), tbuf.at[1, my_slot], sem_t.at[1]).start()
     pltpu.make_async_copy(columns(pv_in, my_slot, HEAD_DIM), vbuf.at[my_slot], sem_v).start()
-    pl.semaphore_wait(barrier, n - 1)
-
-    for far in range(1, blocks):
-        for step in range(KV_HEADS):
-            head = (my_slot + step) % KV_HEADS
-            to = (my_block + far) % blocks * KV_HEADS + head
-            send(columns(q_in, head, WIDTH), qbuf.at[me], send_q, sem_q.at[my_block], to)
-    for step in range(1, KV_HEADS):
-        head = (my_slot + step) % KV_HEADS
+    pltpu.make_async_copy(parents_in, parents, sem_p).start()
+    pl.semaphore_wait(barrier, KV_HEADS - 1 + blocks - 1)
+
+    for block in others:
+        greet(far_ready, block * KV_HEADS + my_slot)
+    for head in heads[1:]:
         to = my_block * KV_HEADS + head
-        send(columns(q_in, head, WIDTH), qbuf.at[me], send_q, sem_q.at[my_block], to)
         send(columns(tk_in, head, HEAD_DIM), tbuf.at[0, my_slot], send_t, sem_t.at[0], to)
         send(columns(pk_in, head, HEAD_DIM), kbuf.at[my_slot], send_k, sem_k, to)
-    for step in range(1, KV_HEADS):
-        head = (my_slot + step) % KV_HEADS
+        send(columns(q_in, head, WIDTH), qbuf.at[me], send_q, sem_q.at[my_block], to)
+    if blocks > 1:
+        pl.semaphore_wait(far_ready, blocks - 1)
+    for block in others:
+        for head in heads:
+            to = block * KV_HEADS + head
+            send(columns(q_in, head, WIDTH), qbuf.at[me], send_q, sem_q.at[my_block], to)
+    for head in heads[1:]:
         to = my_block * KV_HEADS + head
         send(columns(tv_in, head, HEAD_DIM), tbuf.at[1, my_slot], send_t, sem_t.at[1], to)
         send(columns(pv_in, head, HEAD_DIM), vbuf.at[my_slot], send_v, sem_v, to)
 
+    settle(parents, sem_p)
     count = parents.shape[1]
     parent = jnp.broadcast_to(parents[...], (count, count))
     token = lax.broadcasted_iota(jnp.int32, (count, count), 0)
@@ -210,7 +219,7 @@
     return pl.pallas_call(
         functools.partial(kernel, n),
         out_shape=pltpu.VMEM(queries.shape, kind),
-        in_specs=[hbm] * 5 + [vmem],
+        in_specs=[hbm] * 6,
         out_specs=vmem,
         scratch_shapes=[
             pltpu.VMEM((n, local, WIDTH), kind),
@@ -220,7 +229,8 @@
             pltpu.VMEM((n, local, WIDTH + HEAD_DIM), kind),
             pltpu.VMEM((n, local, WIDTH + HEAD_DIM), kind),
             pltpu.VMEM((n * local, KV_HEADS * local), jnp.float32),
-            dma((blocks,)), dma, dma, dma((2,)), dma, dma, dma, dma, dma, dma,
+            pltpu.VMEM((1, n * local), jnp.int32),
+            dma, pltpu.SemaphoreType.REGULAR, dma((blocks,)), dma, dma, dma((2,)), dma, dma, dma, dma, dma, dma,
         ],
         compiler_params=pltpu.CompilerParams(collective_id=0, has_side_effects=True),
         name="tree_attention",

time: 19.6 us -> 18.5 us (0.944)
  Pallas kernels: 18.8 us -> 17.7 us
    pallas_call x1, Pallas kernels: 18.8 us -> 17.7 us  [shards(): pl.pallas_call(functools.partial(kernel, n), out_shape=pltpu.VMEM(queries...]
where the time goes in v3:
time: 18.5 us; the launch traced here: 18.3 us
  Pallas kernels  17.7 us (96%)
  local copies, waits for them, and re-layouts  0.62 us (3%)
    pallas_call x1, Pallas kernels, shards(): pl.pallas_call(functools.partial(kernel, n), out_shape=pltpu.VMEM(queries...  17.7 us
    unnamed x1, local copies, waits for them, and re-layouts  0.62 us

profile of v3, /device:TPU:0, one launch (start us, length us, event | category | flops | bytes accessed | tf_op | source)
XLA Modules:
  0.0 18.3 jit_solution(7563684610770005090)
XLA Ops:
  0.0 17.7 %tree_attention.1 = bf16[8,3072]{1,0:T(8,128)(2,1)S(1)} custom-call(bf16[8,3072]{1,0:T(8,128)(2,1)} %q_in.1, bf16[64,1024]{1,0:T(8,128)(2,1)} %pk_in.1, bf16[64,1024]{1,0:T(8,128)(2,1)} %pv_in.1, bf16[8,1024]{1,0:T(8,128)(2,1)} %tk_in.1, bf16[8,1024]{1,0:T(8,128)(2,1)} %tv_in.1, s32[1,128]{1,0:T(1,128)} %bitcast.1), custom_call_target="tpu_custom_call" | custom-call | tf_op jit(solution)/shard_map/tree_attention/pallas_call | solution.py:219
  17.7 0.6 %copy.8 = bf16[8,3072]{1,0:T(8,128)(2,1)} copy(bf16[8,3072]{1,0:T(8,128)(2,1)S(1)} %tree_attention.1) | data formatting | bytes 98304

commit v4 on v3

--- a/solution.py
+++ b/solution.py
@@ -36,7 +36,8 @@
 def kernel(
     n, q_in, pk_in, pv_in, tk_in, tv_in, parents_in, out,
     qbuf, kbuf, vbuf, tbuf, obuf, rbuf, mask, parents,
-    sem_p, far_ready, sem_q, sem_k, sem_v, sem_t, sem_r, send_q, send_k, send_v, send_t, send_r,
+    q_at, pk_at, pv_at, tk_at, tv_at,
+    sem_p, sem_s, far_ready, sem_q, sem_k, sem_v, sem_t, sem_r, send_q, send_k, send_v, send_t, send_r,
 ):
     me = lax.axis_index("rows")
     local = q_in.shape[0]
@@ -68,31 +69,40 @@
         greet(barrier, block * KV_HEADS + my_slot)
     for head in heads[1:]:
         greet(barrier, my_block * KV_HEADS + head)
+    staged = ((pk_in, pk_at), (tk_in, tk_at), (q_in, q_at), (tv_in, tv_at), (pv_in, pv_at))
+    staging = [
+        pltpu.make_async_copy(here, there, sem_s.at[at])
+        for at, (here, there) in enumerate(staged)
+    ]
+    for copy in staging:
+        copy.start()
     pltpu.make_async_copy(columns(q_in, my_slot, WIDTH), qbuf.at[me], sem_q.at[my_block]).start()
     pltpu.make_async_copy(columns(pk_in, my_slot, HEAD_DIM), kbuf.at[my_slot], sem_k).start()
     pltpu.make_async_copy(columns(tk_in, my_slot, HEAD_DIM), tbuf.at[0, my_slot], sem_t.at[0]).start()
     pltpu.make_async_copy(columns(tv_in, my_slot, HEAD_DIM), tbuf.at[1, my_slot], sem_t.at[1]).start()
     pltpu.make_async_copy(columns(pv_in, my_slot, HEAD_DIM), vbuf.at[my_slot], sem_v).start()
     pltpu.make_async_copy(parents_in, parents, sem_p).start()
+    for copy in staging:
+        copy.wait()
     pl.semaphore_wait(barrier, KV_HEADS - 1 + blocks - 1)
 
     for block in others:
         greet(far_ready, block * KV_HEADS + my_slot)
     for head in heads[1:]:
         to = my_block * KV_HEADS + head
-        send(columns(tk_in, head, HEAD_DIM), tbuf.at[0, my_slot], send_t, sem_t.at[0], to)
-        send(columns(pk_in, head, HEAD_DIM), kbuf.at[my_slot], send_k, sem_k, to)
-        send(columns(q_in, head, WIDTH), qbuf.at[me], send_q, sem_q.at[my_block], to)
+        send(columns(tk_at, head, HEAD_DIM), tbuf.at[0, my_slot], send_t, sem_t.at[0], to)
+        send(columns(pk_at, head, HEAD_DIM), kbuf.at[my_slot], send_k, sem_k, to)
+        send(columns(q_at, head, WIDTH), qbuf.at[me], send_q, sem_q.at[my_block], to)
     if blocks > 1:
         pl.semaphore_wait(far_ready, blocks - 1)
     for block in others:
         for head in heads:
             to = block * KV_HEADS + head
-            send(columns(q_in, head, WIDTH), qbuf.at[me], send_q, sem_q.at[my_block], to)
+            send(columns(q_at, head, WIDTH), qbuf.at[me], send_q, sem_q.at[my_block], to)
     for head in heads[1:]:
         to = my_block * KV_HEADS + head
-        send(columns(tv_in, head, HEAD_DIM), tbuf.at[1, my_slot], send_t, sem_t.at[1], to)
-        send(columns(pv_in, head, HEAD_DIM), vbuf.at[my_slot], send_v, sem_v, to)
+        send(columns(tv_at, head, HEAD_DIM), tbuf.at[1, my_slot], send_t, sem_t.at[1], to)
+        send(columns(pv_at, head, HEAD_DIM), vbuf.at[my_slot], send_v, sem_v, to)
 
     settle(parents, sem_p)
     count = parents.shape[1]
@@ -230,7 +240,10 @@
             pltpu.VMEM((n, local, WIDTH + HEAD_DIM), kind),
             pltpu.VMEM((n * local, KV_HEADS * local), jnp.float32),
             pltpu.VMEM((1, n * local), jnp.int32),
-            dma, pltpu.SemaphoreType.REGULAR, dma((blocks,)), dma, dma, dma((2,)), dma, dma, dma, dma, dma, dma,
+            pltpu.VMEM(queries.shape, kind), pltpu.VMEM(prefix_keys.shape, kind),
+            pltpu.VMEM(prefix_keys.shape, kind), pltpu.VMEM(tree_keys.shape, kind),
+            pltpu.VMEM(tree_keys.shape, kind),
+            dma, dma((5,)), pltpu.SemaphoreType.REGULAR, dma((blocks,)), dma, dma, dma((2,)), dma, dma, dma, dma, dma, dma,
         ],
         compiler_params=pltpu.CompilerParams(collective_id=0, has_side_effects=True),
         name="tree_attention",

time: 18.5 us -> 18.3 us (0.989)
  Pallas kernels: 17.7 us -> 17.5 us
where the time goes in v4:
time: 18.3 us; the launch traced here: 18.2 us
  Pallas kernels  17.5 us (96%)
  local copies, waits for them, and re-layouts  0.62 us (3%)
    pallas_call x1, Pallas kernels, shards(): pl.pallas_call(functools.partial(kernel, n), out_shape=pltpu.VMEM(queries...  17.5 us
    unnamed x1, local copies, waits for them, and re-layouts  0.62 us

profile of v4, /device:TPU:0, one launch (start us, length us, event | category | flops | bytes accessed | tf_op | source)
XLA Modules:
  0.0 18.2 jit_solution(16244435355078864243)
XLA Ops:
  0.0 17.5 %tree_attention.1 = bf16[8,3072]{1,0:T(8,128)(2,1)S(1)} custom-call(bf16[8,3072]{1,0:T(8,128)(2,1)} %q_in.1, bf16[64,1024]{1,0:T(8,128)(2,1)} %pk_in.1, bf16[64,1024]{1,0:T(8,128)(2,1)} %pv_in.1, bf16[8,1024]{1,0:T(8,128)(2,1)} %tk_in.1, bf16[8,1024]{1,0:T(8,128)(2,1)} %tv_in.1, s32[1,128]{1,0:T(1,128)} %bitcast.1), custom_call_target="tpu_custom_call" | custom-call | tf_op jit(solution)/shard_map/tree_attention/pallas_call | solution.py:229
  17.6 0.6 %copy.8 = bf16[8,3072]{1,0:T(8,128)(2,1)} copy(bf16[8,3072]{1,0:T(8,128)(2,1)S(1)} %tree_attention.1) | data formatting | bytes 98304
